TPU v7x, 32 devices: a whole 2x2x4 slice. The times are simulated.
32 devices in a mesh: grp: 4 (over y, core), tm: 8 (over z, x).
Axes of the slice: x: 2, y: 2, z: 4, core: 2. Of those that a mesh axis runs over, the one named last changes fastest.
Arguments:
- wave: bfloat16 [4, 327680], P('grp', 'tm'), may hold values from -6 to 6
- assign: int32 [4, 1024], P('grp', 'tm'), may hold values from 0 to 16383
- w_first: bfloat16 [10, 512], replicated, may hold values from -2 to 2
- w_mid: bfloat16 [4, 1536, 512], replicated, may hold values from -0.15625 to 0.15625
- w_tail: bfloat16 [2, 1024, 512], replicated, may hold values from -0.1875 to 0.1875
- w_proj: bfloat16 [512, 768], replicated, may hold values from -0.25 to 0.25
- centroids: float32 [16384, 768], P('tm'), may hold values from -6 to 6
- prior: float32 [16384], P('tm'), may hold values from 1 to 16
Outputs:
- new_centroids: float32 [16384, 768], P('tm')
- new_counts: float32 [16384], P('tm')
- distortion: float32 [4, 1024], P('grp', 'tm')
All inputs are finite; a program needn't handle non-finite values.
Results may differ from a plain program's by a relative error of at most 0.007.
Values may be sent and summed in bfloat16 or wider, within the bound.
A program may use at most 128 MiB of HBM per device.

v0:
```python
import jax
import jax.numpy as jnp
from jax import lax
from jax.sharding import PartitionSpec as P

HALO = 80
EPS = 1e-05


def passed_along(value, axis, steps):
    count = lax.axis_size(axis)
    leading, last = (max(0, -steps), min(count, count - steps))
    return lax.ppermute(value, axis, [(source, source + steps) for source in range(leading, last)])


def norm_rows(accum):
    row_mean = jnp.mean(accum, axis=-1, keepdims=True)
    centred = accum - row_mean
    spread = jnp.mean(centred * centred, axis=-1, keepdims=True)
    return centred * lax.rsqrt(spread + EPS)


def activate(accum):
    return jax.nn.gelu(norm_rows(accum), approximate=False).astype(jnp.bfloat16)


def first_layer(samples, w_first):
    windows = samples.reshape(-1, 5)
    accum = jnp.dot(windows[:-1], w_first[:5], preferred_element_type=jnp.float32)
    accum = accum + jnp.dot(windows[1:], w_first[5:], preferred_element_type=jnp.float32)
    return activate(accum)


def odd_layer(inputs, weight):
    channels = inputs.shape[1]
    out_len = (inputs.shape[0] - 3) // 2 + 1
    paired = jnp.concatenate([inputs, jnp.zeros((1, channels), inputs.dtype)], axis=0).reshape(
        out_len + 1, 2 * channels
    )
    accum = jnp.dot(paired[:out_len], weight[: 2 * channels], preferred_element_type=jnp.float32)
    accum = accum + jnp.dot(
        paired[1:, :channels], weight[2 * channels :], preferred_element_type=jnp.float32
    )
    return activate(accum)


def even_layer(inputs, weight):
    channels = inputs.shape[1]
    paired = inputs.reshape(inputs.shape[0] // 2, 2 * channels)
    return activate(jnp.dot(paired, weight, preferred_element_type=jnp.float32))


def encode(samples, w_first, w_mid, w_tail):
    hidden = first_layer(samples, w_first)
    for layer_num in range(4):
        hidden = odd_layer(hidden, w_mid[layer_num])
    for layer_num in range(2):
        hidden = even_layer(hidden, w_tail[layer_num])
    return hidden


def project(features, w_proj):
    normed = norm_rows(features.astype(jnp.float32)).astype(jnp.bfloat16)
    return jnp.dot(normed, w_proj, preferred_element_type=jnp.float32).astype(jnp.bfloat16)


def local(wave, assign, w_first, w_mid, w_tail, w_proj, centroids, prior):
    samples = wave[0]
    tail_part = passed_along(samples[:HALO], "tm", -1)
    features = encode(jnp.concatenate([samples, tail_part]), w_first, w_mid, w_tail)
    own_labels = assign[0]
    shard_len = centroids.shape[0]
    feat_width = centroids.shape[1]
    first_id = lax.axis_index("tm") * shard_len
    centroid_ids = first_id + jnp.arange(shard_len, dtype=jnp.int32)
    rounded = lax.optimization_barrier(centroids.astype(jnp.bfloat16))
    widened = rounded.astype(jnp.float32)
    centroid_sq = jnp.sum(widened * widened, axis=1)
    frames = project(features, w_proj)
    accumulate_frames = lax.all_gather(frames, "tm", axis=0, tiled=True)
    labels = lax.all_gather(own_labels, "tm", axis=0, tiled=True)
    one_hot = labels[None, :] == centroid_ids[:, None]
    hot_rows = labels[:, None] == centroid_ids[None, :]
    hot_sums = jnp.dot(
        one_hot.astype(jnp.bfloat16), accumulate_frames, preferred_element_type=jnp.float32
    )
    counts = jnp.sum(one_hot.astype(jnp.float32), axis=1)
    products = jnp.einsum(
        "rd,kd->rk", accumulate_frames, rounded, preferred_element_type=jnp.float32
    )
    frame_wide = accumulate_frames.astype(jnp.float32)
    squares = jnp.sum(frame_wide * frame_wide, axis=1)
    is_owner = (labels >= first_id) & (labels < first_id + shard_len)
    picked = jnp.sum(jnp.where(hot_rows, centroid_sq[None, :] - 2.0 * products, 0.0), axis=1)
    own_term = jnp.where(is_owner, squares + picked, 0.0)
    term_sums = lax.psum_scatter(own_term, "tm", scatter_dimension=0, tiled=True)
    distortion = (term_sums / feat_width)[None, :]
    total_sums, total_counts = (
        lax.psum(hot_sums.astype(jnp.bfloat16), "grp").astype(jnp.float32),
        lax.psum(counts.astype(jnp.bfloat16), "grp").astype(jnp.float32),
    )
    new_counts = prior + total_counts
    new_centroids = (prior[:, None] * centroids + total_sums) / new_counts[:, None]
    return (new_centroids, new_counts, distortion)


def solution(mesh):
    return jax.shard_map(
        local,
        mesh=mesh,
        in_specs=(P("grp", "tm"), P("grp", "tm"), P(), P(), P(), P(), P("tm", None), P("tm")),
        out_specs=(P("tm", None), P("tm"), P("grp", "tm")),
        check_vma=False,
    )
```

profile of v0, /device:TPU:0, one launch (start us, length us, event | category | flops | bytes accessed | tf_op | source)
XLA Modules:
  0.0 410.5 jit_solution(17534476603627418723)
XLA Ops:
  7.2 0.7 slice_bitcast_fusion
  8.0 1.3 collective-permute-start
  9.2 1.4 reduce
  10.6 3.7 collective-permute-done
  14.3 0.1 slice_maximum_fusion
  14.4 4.5 %slice.152 = bf16[8207,5]{1,0:T(8,128)(2,1)S(1)} reshape(bf16[41035]{0:T(1024)(128)(2,1)S(1)} %get-tuple-element.8) | data formatting | bytes 164140 | tf_op jit(solution)/shard_map/slice | solution.py:30
  19.0 5.9 %slice.149 = bf16[8207,5]{1,0:T(8,128)(2,1)} reshape(bf16[41035]{0:T(1024)(128)(2,1)S(1)} %get-tuple-element.7) | data formatting | bytes 164140 | tf_op jit(solution)/shard_map/slice | solution.py:29
  24.8 8.0 %fusion.115 = f32[8207,512]{1,0:T(8,128)} fusion(bf16[8207,5]{1,0:T(8,128)(2,1)S(1)} %slice.152, bf16[10,512]{1,0:T(8,128)(2,1)S(1)} %copy-done.9), kind=kOutput, calls=%fused_computation.204 | convolution fusion | flops 42019840 | bytes 18917376 | tf_op jit(solution)/shard_map/dot_general | solution.py:30
  32.9 10.8 %fusion.121 = (f32[8207]{0:T(1024)S(1)}, f32[8207,512]{1,0:T(8,128)}) fusion(f32[8207,512]{1,0:T(8,128)} %fusion.115, bf16[8207,5]{1,0:T(8,128)(2,1)S(1)} %copy-done.5, bf16[10,512]{1,0:T(8,128)(2,1)S(1)} %copy-done.9), kind=kOutput, calls=%fused_computation.223 | convolution fusion | flops 50415600 | bytes 35758140 | tf_op jit(solution)/shard_map/dot_general | solution.py:29
  43.7 10.4 %multiply_reduce_fusion = f32[8207]{0:T(1024)S(1)} fusion(f32[8207,512]{1,0:T(8,128)} %get-tuple-element.10, f32[8207]{0:T(1024)S(1)} %broadcast_multiply_fusion), kind=kLoop, calls=%fused_computation.17 | loop fusion | flops 12597745 | bytes 16873592 | tf_op jit(solution)/shard_map/reduce_sum | solution.py:19
  54.1 0.3 copy-done.1
  54.4 45.7 %fusion.2 = bf16[8207,512]{1,0:T(8,128)(2,1)} fusion(f32[8207,512]{1,0:T(8,128)S(1)} %copy-done.1, f32[8207]{0:T(1024)S(1)} %add_rsqrt_fusion, f32[8207]{0:T(1024)S(1)} %broadcast_multiply_fusion), kind=kLoop, calls=%fused_computation.3 | loop fusion | flops 281532928 | bytes 25277560 | tf_op jit(solution)/shard_map/convert_element_type | solution.py:24
  100.1 13.0 %slice.155 = bf16[4103,1024]{1,0:T(8,128)(2,1)} reshape(bf16[8206,512]{1,0:T(8,128)(2,1)} %bitcast.63) | data formatting | bytes 16805888 | tf_op jit(solution)/shard_map/slice | solution.py:40
  113.1 8.0 %concatenate.16 = bf16[8208,512]{1,0:T(8,128)(2,1)} pad(bf16[8207,512]{1,0:T(8,128)(2,1)} %fusion.2, bf16[]{:T(256)} %constant.70.clone.1), padding=0_1x0_0 | pad | bytes 16808962 | tf_op jit(solution)/shard_map/concatenate | solution.py:37
  121.1 13.0 %reshape.165 = bf16[4104,1024]{1,0:T(8,128)(2,1)} reshape(bf16[8208,512]{1,0:T(8,128)(2,1)} %concatenate.16) | data formatting | bytes 16809984 | tf_op jit(solution)/shard_map/reshape | solution.py:37
  134.1 7.4 %fusion.64 = f32[4103,512]{1,0:T(8,128)S(1)} fusion(bf16[4103,1024]{1,0:T(8,128)(2,1)} %slice.155, bf16[4,1536,512]{2,1,0:T(8,128)(2,1)} %param.11), kind=kOutput, calls=%fused_computation.114 | convolution fusion | flops 4302307328 | bytes 17856512 | tf_op jit(solution)/shard_map/dot_general | solution.py:40
  141.6 3.7 fusion.122
  145.3 1.7 multiply_reduce_fusion.1
  147.0 22.3 %fusion.14 = bf16[4103,512]{1,0:T(8,128)(2,1)S(1)} fusion(f32[4103,512]{1,0:T(8,128)S(1)} %get-tuple-element.12, f32[4103]{0:T(1024)S(1)} %add_rsqrt_fusion.1, f32[4103]{0:T(1024)S(1)} %broadcast_multiply_fusion.1), kind=kLoop, calls=%fused_computation.27 | loop fusion | flops 140749312 | bytes 12637240 | tf_op jit(solution)/shard_map/convert_element_type | solution.py:24
  169.4 1.9 copy-done.2
  171.3 2.2 concatenate.17
  173.6 7.2 %slice.162 = bf16[2051,1024]{1,0:T(8,128)(2,1)} reshape(bf16[4102,512]{1,0:T(8,128)(2,1)} %bitcast.64) | data formatting | bytes 8400896 | tf_op jit(solution)/shard_map/slice | solution.py:40
  180.7 6.8 %fusion.62 = f32[2051,512]{1,0:T(8,128)} fusion(bf16[2051,1024]{1,0:T(8,128)(2,1)} %slice.162, bf16[4,1536,512]{2,1,0:T(8,128)(2,1)} %param.11), kind=kOutput, calls=%fused_computation.112 | convolution fusion | flops 2150629376 | bytes 9459712 | tf_op jit(solution)/shard_map/dot_general | solution.py:40
  187.5 7.2 %reshape.166 = bf16[2052,1024]{1,0:T(8,128)(2,1)} reshape(bf16[4104,512]{1,0:T(8,128)(2,1)} %concatenate.17) | data formatting | bytes 8404992 | tf_op jit(solution)/shard_map/reshape | solution.py:37
  194.7 4.5 %fusion.123 = (f32[2051]{0:T(1024)S(1)}, f32[2051,512]{1,0:T(8,128)S(1)}) fusion(f32[2051,512]{1,0:T(8,128)} %fusion.62, bf16[4,1536,512]{2,1,0:T(8,128)(2,1)} %param.11, bf16[2052,1024]{1,0:T(8,128)(2,1)} %reshape.166), kind=kOutput, calls=%fused_computation.225 | convolution fusion | flops 1077412864 | bytes 11048972 | tf_op jit(solution)/shard_map/dot_general | solution.py:41
  199.2 0.9 multiply_reduce_fusion.3
  200.1 11.7 %fusion.25 = bf16[2051,512]{1,0:T(8,128)(2,1)S(1)} fusion(f32[2051,512]{1,0:T(8,128)S(1)} %get-tuple-element.14, f32[2051]{0:T(1024)S(1)} %add_rsqrt_fusion.2, f32[2051]{0:T(1024)S(1)} %broadcast_multiply_fusion.2), kind=kLoop, calls=%fused_computation.53 | loop fusion | flops 70357504 | bytes 6317080 | tf_op jit(solution)/shard_map/convert_element_type | solution.py:24
  211.8 1.4 concatenate.18
  213.3 2.0 slice.169
  215.3 4.6 %fusion.60 = f32[1025,512]{1,0:T(8,128)} fusion(bf16[1025,1024]{1,0:T(8,128)(2,1)} %slice.169, bf16[4,1536,512]{2,1,0:T(8,128)(2,1)} %param.11), kind=kOutput, calls=%fused_computation.110 | convolution fusion | flops 1074790400 | bytes 5261312 | tf_op jit(solution)/shard_map/dot_general | solution.py:40
  219.9 2.0 reshape.167
  221.9 2.9 fusion.124
  224.8 0.5 multiply_reduce_fusion.5
  225.3 5.7 %fusion.41 = bf16[1025,512]{1,0:T(8,128)(2,1)S(1)} fusion(f32[1025,512]{1,0:T(8,128)S(1)} %get-tuple-element.16, f32[1025]{0:T(1024)S(1)} %add_rsqrt_fusion.3, f32[1025]{0:T(1024)S(1)} %broadcast_multiply_fusion.3), kind=kLoop, calls=%fused_computation.79 | loop fusion | flops 35161600 | bytes 3157000 | tf_op jit(solution)/shard_map/convert_element_type | solution.py:24
  231.2 1.2 slice.176
  232.3 3.3 fusion.58
  235.6 0.3 reshape.168
  236.0 1.9 fusion.125
  237.9 0.2 multiply_reduce_fusion.6
  238.0 2.6 fusion.53
  240.6 0.2 copy.13
  240.8 0.2 reshape.169
  241.0 1.7 fusion.126
  242.8 0.2 multiply_reduce_fusion.7
  243.0 1.3 fusion.81
  244.3 0.1 reshape.170
  244.4 1.6 fusion.127
  246.1 0.2 multiply_reduce_fusion.8
  246.3 0.8 convert_reduce_fusion
  247.0 0.2 fusion.100
  247.2 1.0 convolution_convert_fusion
  248.3 19.6 %all-gather = s32[1,1024]{1,0:T(1,128)S(1)} all-gather(s32[1,128]{1,0:T(1,128)S(1)} %copy-done.10), channel_id=2, replica_groups=mesh['grp'=4,'tm'=8] {'tm'}, dimensions={1}, use_global_device_ids=true | all-gather | bytes 4608 | tf_op jit(solution)/shard_map/all_gather | solution.py:81
  267.9 26.3 %all-gather.3.cloned.1.call-done = bf16[1024,768]{1,0:T(8,128)(2,1)} async-done(((bf16[128,768]{1,0:T(8,128)(2,1)}), bf16[1024,768]{1,0:T(8,128)(2,1)}) %all-gather.3.cloned.1.call-update) | async-done | bytes 1572880 | tf_op jit(solution)/shard_map/all_gather | solution.py:80
  294.2 6.3 %fusion.36 = bf16[2048,768]{1,0:T(8,128)(2,1)} fusion(bf16[1024,768]{1,0:T(8,128)(2,1)} %all-gather.3.cloned.1.call-done, s32[1024]{0:T(1024)S(1)} %bitcast.66, s32[2048]{0:T(1024)S(1)} %iota_add_fusion), kind=kOutput, calls=%fused_computation.74 | convolution fusion | flops 3224895488 | bytes 4730880 | tf_op jit(solution)/shard_map/dot_general | solution.py:84
  300.6 0.6 dynamic-slice
  301.9 1.1 fusion.22
  303.0 6.4 %psum.15 = bf16[2048]{0:T(1024)(128)(2,1)S(1)} all-reduce(bf16[2048]{0:T(1024)(128)(2,1)S(1)} %fusion.22), channel_id=1, replica_groups=mesh['grp'=4,'tm'=8] {'grp'}, use_global_device_ids=true, to_apply=%region_18.0 | all-reduce | flops 2048 | bytes 8192 | tf_op jit(solution)/shard_map/psum | solution.py:100
  309.4 0.4 multiply_reduce_fusion.4
  309.8 58.2 %all-reduce.7.cloned.1.call-done = bf16[2048,768]{1,0:T(8,128)(2,1)} async-done(((bf16[2048,768]{1,0:T(8,128)(2,1)}), bf16[2048,768]{1,0:T(8,128)(2,1)}) %all-reduce.7.cloned.1.call-update) | async-done | bytes 3145744 | tf_op jit(solution)/shard_map/psum | solution.py:99
  368.1 8.7 %fusion.120 = (bf16[2048,768]{1,0:T(8,128)(2,1)S(1)}, f32[2048,768]{1,0:T(8,128)}) fusion(f32[2048,768]{1,0:T(8,128)} %param.14, f32[2048]{0:T(1024)S(1)} %convert_add_fusion, bf16[2048,768]{1,0:T(8,128)(2,1)} %all-reduce.7.cloned.1.call-done, f32[2048]{0:T(1024)S(1)} %copy-done.7), kind=kLoop, calls=%fused_computation.222 | loop fusion | flops 7864320 | bytes 18890752 | tf_op jit(solution)/shard_map/convert_element_type | solution.py:76
  376.8 0.7 multiply_reduce_fusion.2
  377.4 4.0 select_reduce_fusion
  381.5 21.4 %all-reduce.4 = f32[1024]{0:T(1024)S(1)} all-reduce(f32[1024]{0:T(1024)S(1)} %add_select_fusion), channel_id=3, replica_groups=mesh['grp'=4,'tm'=8] {'tm'}, use_global_device_ids=true, to_apply=%region_22.23.clone | all-reduce | flops 1024 | bytes 8192
  402.9 0.6 fusion.118
  (47 shorter events, 0.4 us)
Async XLA Ops:
  7.2 240.1 %copy-start = (bf16[512,768]{1,0:T(8,128)(2,1)S(1)}, bf16[512,768]{1,0:T(8,128)(2,1)}, u32[]{:S(2)}) copy-start(bf16[512,768]{1,0:T(8,128)(2,1)} %param.13) | copy-start | bytes 2359300
  7.2 17.6 %copy-start.9 = (bf16[10,512]{1,0:T(8,128)(2,1)S(1)}, bf16[10,512]{1,0:T(8,128)(2,1)}, u32[]{:S(2)}) copy-start(bf16[10,512]{1,0:T(8,128)(2,1)} %param.10) | copy-start | bytes 30724
  7.2 287.0 %all-gather.3.cloned.1.call-start = ((), (), s32[]{:S(2)}) async-start(), calls=%async_computation | async-start | bytes 1769472 | tf_op jit(solution)/shard_map/all_gather | solution.py:80
  8.0 6.3 %collective-permute-start = (bf16[80]{0:T(256)(128)(2,1)S(1)}, bf16[80]{0:T(256)(128)(2,1)S(1)}, u32[]{:S(2)}, u32[]{:S(2)}) collective-permute-start(bf16[80]{0:T(256)(128)(2,1)S(1)} %slice_bitcast_fusion), channel_id=1, source_target_pairs={{1,0},{2,1},{3,2},{4,3},{5,4},{6,5},{7,6},{9,8},{10,9},{11,10},{12... | collective-permute-start | bytes 488 | tf_op jit(solution)/shard_map/ppermute | solution.py:13
  24.8 8.0 %copy-start.5 = (bf16[8207,5]{1,0:T(8,128)(2,1)S(1)}, bf16[8207,5]{1,0:T(8,128)(2,1)}, u32[]{:S(2)}) copy-start(bf16[8207,5]{1,0:T(8,128)(2,1)} %slice.149) | copy-start | bytes 246214
  43.7 10.7 %copy-start.1 = (f32[8207,512]{1,0:T(8,128)S(1)}, f32[8207,512]{1,0:T(8,128)}, u32[]{:S(2)}) copy-start(f32[8207,512]{1,0:T(8,128)} %get-tuple-element.10) | copy-start | bytes 50423812
  134.1 7.4 %copy-start.3 = (bf16[4104,1024]{1,0:T(8,128)(2,1)S(1)}, bf16[4104,1024]{1,0:T(8,128)(2,1)}, u32[]{:S(2)}) copy-start(bf16[4104,1024]{1,0:T(8,128)(2,1)} %reshape.165) | copy-start | bytes 25214980
  169.4 1.9 copy-start.2
  215.3 4.6 %copy-start.4 = (bf16[2052,512]{1,0:T(8,128)(2,1)S(1)}, bf16[2052,512]{1,0:T(8,128)(2,1)}, u32[]{:S(2)}) copy-start(bf16[2052,512]{1,0:T(8,128)(2,1)} %concatenate.18) | copy-start | bytes 6303748
  241.0 7.3 %copy-start.10 = (s32[1,128]{1,0:T(1,128)S(1)}, s32[1,128]{1,0:T(1,128)}, u32[]{:S(2)}) copy-start(s32[1,128]{1,0:T(1,128)} %param.9) | copy-start | bytes 1540
  248.3 119.8 %all-reduce.7.cloned.1.call-start = ((), (), s32[]{:S(2)}) async-start(), calls=%async_computation.1 | async-start | bytes 6291456 | tf_op jit(solution)/shard_map/psum | solution.py:99
  294.2 6.4 %copy-start.11 = (u32[32]{0:T(128)S(1)}, u32[32]{0:T(128)}, u32[]{:S(2)}) copy-start(u32[32]{0:T(128)} %constant.30) | copy-start | bytes 388
  294.2 15.2 %copy-start.7 = (f32[2048]{0:T(1024)S(1)}, f32[2048]{0:T(1024)}, u32[]{:S(2)}) copy-start(f32[2048]{0:T(1024)} %param.15) | copy-start | bytes 24580
  300.6 8.8 %copy-start.6 = (bf16[1024,768]{1,0:T(8,128)(2,1)S(1)}, bf16[1024,768]{1,0:T(8,128)(2,1)}, u32[]{:S(2)}) copy-start(bf16[1024,768]{1,0:T(8,128)(2,1)} %all-gather.3.cloned.1.call-done) | copy-start | bytes 4718596
  309.4 67.3 %copy-start.8 = (f32[2048]{0:T(1024)}, f32[2048]{0:T(1024)S(1)}, u32[]{:S(2)}) copy-start(f32[2048]{0:T(1024)S(1)} %convert_add_fusion) | copy-start | bytes 24580
Sparse Core Ops, SparseCore 0:
  248.4 45.8 all-gather.2
  300.7 67.2 all-reduce.6
where the time goes:
time: 418 us; the launch traced here: 410 us
  other arithmetic  117 us (28%)
  waiting for transfers between devices  88.3 us (21%)
  local copies, waits for them, and re-layouts  72.2 us (17%)
  matrix products  68.8 us (16%)
  blocking collectives  47.4 us (11%)
  between operations  15.2 us (4%)
    convert_element_type x6, other arithmetic, activate(): return jax.nn.gelu(norm_rows(accum), approximate=False).astype(jnp.bfloat16)  89.3 us
    psum x1, waiting for transfers between devices, local(): lax.psum(hot_sums.astype(jnp.bfloat16), 'grp').astype(jnp.float32)  58.2 us
    all_gather x1, waiting for transfers between devices, local(): accumulate_frames = lax.all_gather(frames, 'tm', axis=0, tiled=True)  26.3 us
    slice x5, local copies, waits for them, and re-layouts, odd_layer(): paired[:out_len]  23.4 us
    reshape x4, local copies, waits for them, and re-layouts, odd_layer(): jnp.concatenate([inputs, jnp.zeros((1, channels), inputs.dtype)], axis=0)  22.5 us
    dot_general x4, matrix products, odd_layer(): jnp.dot(paired[:out_len], weight[:2 * channels], preferred_element_type=j...  22.1 us
    unnamed x1, blocking collectives  21.4 us
    all_gather x1, blocking collectives, local(): labels = lax.all_gather(own_labels, 'tm', axis=0, tiled=True)  19.6 us
  transfers between devices with their start and end apart: 3, of which 3 were waited for; matrix products, arithmetic and copies ran while one was open for 1% of the time, Pallas kernels for 0%

commit v1 on v0

--- a/solution.py
+++ b/solution.py
@@ -5,6 +5,11 @@
 
 HALO = 80
 EPS = 1e-05
+
+
+def add_all(x, name):
+    parts = lax.all_gather(x, name)
+    return jnp.sum(parts, axis=0)
 
 
 def passed_along(value, axis, steps):
@@ -96,7 +101,7 @@
     term_sums = lax.psum_scatter(own_term, "tm", scatter_dimension=0, tiled=True)
     distortion = (term_sums / feat_width)[None, :]
     total_sums, total_counts = (
-        lax.psum(hot_sums.astype(jnp.bfloat16), "grp").astype(jnp.float32),
+        add_all(hot_sums.astype(jnp.bfloat16), "grp").astype(jnp.float32),
         lax.psum(counts.astype(jnp.bfloat16), "grp").astype(jnp.float32),
     )
     new_counts = prior + total_counts

time: 418 us -> 441 us (1.055)
  waiting for transfers between devices: 88.3 us -> 102 us
  other arithmetic: 117 us -> 127 us
    all_gather x0 -> x1, waiting for transfers between devices: none -> 72.3 us  [add_all(): parts = lax.all_gather(x, name)]
    psum x1 -> x0, waiting for transfers between devices: 58.2 us -> none  [local(): lax.psum(hot_sums.astype(jnp.bfloat16), 'grp').astype(jnp.float32)]
    reduce_sum x0 -> x1, other arithmetic: none -> 8.97 us  [add_all(): return jnp.sum(parts, axis=0)]
where the time goes in v1:
time: 441 us; the launch traced here: 433 us
  other arithmetic  127 us (29%)
  waiting for transfers between devices  102 us (23%)
  local copies, waits for them, and re-layouts  72.2 us (16%)
  matrix products  68.7 us (16%)
  blocking collectives  46.9 us (11%)
  between operations  15.3 us (3%)
    convert_element_type x6, other arithmetic, activate(): return jax.nn.gelu(norm_rows(accum), approximate=False).astype(jnp.bfloat16)  89.3 us
    all_gather x1, waiting for transfers between devices, add_all(): parts = lax.all_gather(x, name)  72.3 us
    all_gather x1, waiting for transfers between devices, local(): accumulate_frames = lax.all_gather(frames, 'tm', axis=0, tiled=True)  26.3 us
    slice x5, local copies, waits for them, and re-layouts, odd_layer(): paired[:out_len]  23.4 us
    reshape x4, local copies, waits for them, and re-layouts, odd_layer(): jnp.concatenate([inputs, jnp.zeros((1, channels), inputs.dtype)], axis=0)  22.5 us
    dot_general x4, matrix products, odd_layer(): jnp.dot(paired[:out_len], weight[:2 * channels], preferred_element_type=j...  22.1 us
    unnamed x1, blocking collectives  21.4 us
    all_gather x1, blocking collectives, local(): labels = lax.all_gather(own_labels, 'tm', axis=0, tiled=True)  19.6 us
  transfers between devices with their start and end apart: 3, of which 3 were waited for; matrix products, arithmetic and copies ran while one was open for 1% of the time, Pallas kernels for 0%

profile of v1, /device:TPU:0, one launch (start us, length us, event | category | flops | bytes accessed | tf_op | source)
XLA Modules:
  0.0 433.4 jit_solution(18312388292109319015)
XLA Ops:
  7.2 0.7 slice_bitcast_fusion
  8.0 1.3 collective-permute-start
  9.2 1.4 reduce.1
  10.6 3.7 collective-permute-done
  14.3 0.1 slice_maximum_fusion
  14.4 4.5 %slice.152 = bf16[8207,5]{1,0:T(8,128)(2,1)S(1)} reshape(bf16[41035]{0:T(1024)(128)(2,1)S(1)} %get-tuple-element.8) | data formatting | bytes 164140 | tf_op jit(solution)/shard_map/slice | solution.py:35
  19.0 5.9 %slice.149 = bf16[8207,5]{1,0:T(8,128)(2,1)} reshape(bf16[41035]{0:T(1024)(128)(2,1)S(1)} %get-tuple-element.7) | data formatting | bytes 164140 | tf_op jit(solution)/shard_map/slice | solution.py:34
  24.8 8.0 %fusion.115 = f32[8207,512]{1,0:T(8,128)} fusion(bf16[8207,5]{1,0:T(8,128)(2,1)S(1)} %slice.152, bf16[10,512]{1,0:T(8,128)(2,1)S(1)} %copy-done.9), kind=kOutput, calls=%fused_computation.204 | convolution fusion | flops 42019840 | bytes 18917376 | tf_op jit(solution)/shard_map/dot_general | solution.py:35
  32.9 10.8 %fusion.121 = (f32[8207]{0:T(1024)S(1)}, f32[8207,512]{1,0:T(8,128)}) fusion(f32[8207,512]{1,0:T(8,128)} %fusion.115, bf16[8207,5]{1,0:T(8,128)(2,1)S(1)} %copy-done.5, bf16[10,512]{1,0:T(8,128)(2,1)S(1)} %copy-done.9), kind=kOutput, calls=%fused_computation.223 | convolution fusion | flops 50415600 | bytes 35758140 | tf_op jit(solution)/shard_map/dot_general | solution.py:34
  43.7 10.4 %multiply_reduce_fusion = f32[8207]{0:T(1024)S(1)} fusion(f32[8207,512]{1,0:T(8,128)} %get-tuple-element.10, f32[8207]{0:T(1024)S(1)} %broadcast_multiply_fusion), kind=kLoop, calls=%fused_computation.17 | loop fusion | flops 12597745 | bytes 16873592 | tf_op jit(solution)/shard_map/reduce_sum | solution.py:24
  54.1 0.3 copy-done.1
  54.4 45.7 %fusion.2 = bf16[8207,512]{1,0:T(8,128)(2,1)} fusion(f32[8207,512]{1,0:T(8,128)S(1)} %copy-done.1, f32[8207]{0:T(1024)S(1)} %add_rsqrt_fusion, f32[8207]{0:T(1024)S(1)} %broadcast_multiply_fusion), kind=kLoop, calls=%fused_computation.3 | loop fusion | flops 281532928 | bytes 25277560 | tf_op jit(solution)/shard_map/convert_element_type | solution.py:29
  100.0 13.0 %slice.155 = bf16[4103,1024]{1,0:T(8,128)(2,1)} reshape(bf16[8206,512]{1,0:T(8,128)(2,1)} %bitcast.64) | data formatting | bytes 16805888 | tf_op jit(solution)/shard_map/slice | solution.py:45
  113.1 8.0 %concatenate.16 = bf16[8208,512]{1,0:T(8,128)(2,1)} pad(bf16[8207,512]{1,0:T(8,128)(2,1)} %fusion.2, bf16[]{:T(256)} %constant.70.clone.1), padding=0_1x0_0 | pad | bytes 16808962 | tf_op jit(solution)/shard_map/concatenate | solution.py:42
  121.1 13.0 %reshape.165 = bf16[4104,1024]{1,0:T(8,128)(2,1)} reshape(bf16[8208,512]{1,0:T(8,128)(2,1)} %concatenate.16) | data formatting | bytes 16809984 | tf_op jit(solution)/shard_map/reshape | solution.py:42
  134.1 7.4 %fusion.64 = f32[4103,512]{1,0:T(8,128)S(1)} fusion(bf16[4103,1024]{1,0:T(8,128)(2,1)} %slice.155, bf16[4,1536,512]{2,1,0:T(8,128)(2,1)} %param.11), kind=kOutput, calls=%fused_computation.114 | convolution fusion | flops 4302307328 | bytes 17856512 | tf_op jit(solution)/shard_map/dot_general | solution.py:45
  141.5 3.8 fusion.122
  145.3 1.7 multiply_reduce_fusion.1
  147.0 22.3 %fusion.14 = bf16[4103,512]{1,0:T(8,128)(2,1)S(1)} fusion(f32[4103,512]{1,0:T(8,128)S(1)} %get-tuple-element.12, f32[4103]{0:T(1024)S(1)} %add_rsqrt_fusion.1, f32[4103]{0:T(1024)S(1)} %broadcast_multiply_fusion.1), kind=kLoop, calls=%fused_computation.27 | loop fusion | flops 140749312 | bytes 12637240 | tf_op jit(solution)/shard_map/convert_element_type | solution.py:29
  169.4 1.9 copy-done.2
  171.3 2.2 concatenate.17
  173.5 7.2 %slice.162 = bf16[2051,1024]{1,0:T(8,128)(2,1)} reshape(bf16[4102,512]{1,0:T(8,128)(2,1)} %bitcast.65) | data formatting | bytes 8400896 | tf_op jit(solution)/shard_map/slice | solution.py:45
  180.7 6.8 %fusion.62 = f32[2051,512]{1,0:T(8,128)} fusion(bf16[2051,1024]{1,0:T(8,128)(2,1)} %slice.162, bf16[4,1536,512]{2,1,0:T(8,128)(2,1)} %param.11), kind=kOutput, calls=%fused_computation.112 | convolution fusion | flops 2150629376 | bytes 9459712 | tf_op jit(solution)/shard_map/dot_general | solution.py:45
  187.5 7.2 %reshape.166 = bf16[2052,1024]{1,0:T(8,128)(2,1)} reshape(bf16[4104,512]{1,0:T(8,128)(2,1)} %concatenate.17) | data formatting | bytes 8404992 | tf_op jit(solution)/shard_map/reshape | solution.py:42
  194.6 4.5 %fusion.123 = (f32[2051]{0:T(1024)S(1)}, f32[2051,512]{1,0:T(8,128)S(1)}) fusion(f32[2051,512]{1,0:T(8,128)} %fusion.62, bf16[4,1536,512]{2,1,0:T(8,128)(2,1)} %param.11, bf16[2052,1024]{1,0:T(8,128)(2,1)} %reshape.166), kind=kOutput, calls=%fused_computation.225 | convolution fusion | flops 1077412864 | bytes 11048972 | tf_op jit(solution)/shard_map/dot_general | solution.py:46
  199.2 0.9 multiply_reduce_fusion.3
  200.1 11.7 %fusion.25 = bf16[2051,512]{1,0:T(8,128)(2,1)S(1)} fusion(f32[2051,512]{1,0:T(8,128)S(1)} %get-tuple-element.14, f32[2051]{0:T(1024)S(1)} %add_rsqrt_fusion.2, f32[2051]{0:T(1024)S(1)} %broadcast_multiply_fusion.2), kind=kLoop, calls=%fused_computation.53 | loop fusion | flops 70357504 | bytes 6317080 | tf_op jit(solution)/shard_map/convert_element_type | solution.py:29
  211.8 1.4 concatenate.18
  213.2 2.0 slice.169
  215.2 4.6 %fusion.60 = f32[1025,512]{1,0:T(8,128)} fusion(bf16[1025,1024]{1,0:T(8,128)(2,1)} %slice.169, bf16[4,1536,512]{2,1,0:T(8,128)(2,1)} %param.11), kind=kOutput, calls=%fused_computation.110 | convolution fusion | flops 1074790400 | bytes 5261312 | tf_op jit(solution)/shard_map/dot_general | solution.py:45
  219.9 2.0 reshape.167
  221.9 2.9 fusion.124
  224.8 0.5 multiply_reduce_fusion.5
  225.3 5.7 %fusion.41 = bf16[1025,512]{1,0:T(8,128)(2,1)S(1)} fusion(f32[1025,512]{1,0:T(8,128)S(1)} %get-tuple-element.16, f32[1025]{0:T(1024)S(1)} %add_rsqrt_fusion.3, f32[1025]{0:T(1024)S(1)} %broadcast_multiply_fusion.3), kind=kLoop, calls=%fused_computation.79 | loop fusion | flops 35161600 | bytes 3157000 | tf_op jit(solution)/shard_map/convert_element_type | solution.py:29
  231.1 1.2 slice.176
  232.3 3.3 fusion.58
  235.6 0.3 reshape.168
  235.9 1.9 fusion.125
  237.8 0.2 multiply_reduce_fusion.6
  238.0 2.6 fusion.53
  240.6 0.2 copy.13
  240.8 0.2 reshape.169
  241.0 1.7 fusion.126
  242.8 0.2 multiply_reduce_fusion.7
  243.0 1.3 fusion.81
  244.4 1.6 fusion.127
  246.0 0.2 multiply_reduce_fusion.8
  246.2 0.8 convert_reduce_fusion
  247.0 0.2 fusion.100
  247.2 1.0 convolution_convert_fusion
  248.3 19.6 %all-gather = s32[1,1024]{1,0:T(1,128)S(1)} all-gather(s32[1,128]{1,0:T(1,128)S(1)} %copy-done.10), channel_id=2, replica_groups=mesh['grp'=4,'tm'=8] {'tm'}, dimensions={1}, use_global_device_ids=true | all-gather | bytes 4608 | tf_op jit(solution)/shard_map/all_gather | solution.py:86
  267.9 26.3 %all-gather.5.cloned.1.call-done = bf16[1024,768]{1,0:T(8,128)(2,1)} async-done(((bf16[128,768]{1,0:T(8,128)(2,1)}), bf16[1024,768]{1,0:T(8,128)(2,1)}) %all-gather.5.cloned.1.call-update) | async-done | bytes 1572880 | tf_op jit(solution)/shard_map/all_gather | solution.py:85
  294.2 6.3 %fusion.36 = bf16[2048,768]{1,0:T(8,128)(2,1)} fusion(bf16[1024,768]{1,0:T(8,128)(2,1)} %all-gather.5.cloned.1.call-done, s32[1024]{0:T(1024)S(1)} %bitcast.68, s32[2048]{0:T(1024)S(1)} %iota_add_fusion), kind=kOutput, calls=%fused_computation.74 | convolution fusion | flops 3224895488 | bytes 4730880 | tf_op jit(solution)/shard_map/dot_general | solution.py:89
  300.6 0.6 dynamic-slice
  301.9 1.1 fusion.22
  303.0 6.0 %psum.7 = bf16[2048]{0:T(1024)(128)(2,1)S(1)} all-reduce(bf16[2048]{0:T(1024)(128)(2,1)S(1)} %fusion.22), channel_id=1, replica_groups=mesh['grp'=4,'tm'=8] {'grp'}, use_global_device_ids=true, to_apply=%region_18.0 | all-reduce | flops 2048 | bytes 8192 | tf_op jit(solution)/shard_map/psum | solution.py:105
  309.0 0.4 multiply_reduce_fusion.4
  309.3 72.3 %all-gather.7.cloned.1.call-done = bf16[8192,768]{1,0:T(8,128)(2,1)} async-done(((bf16[2048,768]{1,0:T(8,128)(2,1)}), bf16[8192,768]{1,0:T(8,128)(2,1)}) %all-gather.7.cloned.1.call-update) | async-done | bytes 12582928 | tf_op jit(solution)/shard_map/all_gather | solution.py:11
  381.7 9.0 %reduce_sum.208 = bf16[2048,768]{1,0:T(8,128)(2,1)} reduce(bf16[4,2048,768]{2,1,0:T(8,128)(2,1)} %bitcast.67, bf16[]{:T(256)} %constant.70.clone.1), dimensions={0}, to_apply=%region_16.0 | reduce | flops 4718592 | bytes 15728642 | tf_op jit(solution)/shard_map/reduce_sum | solution.py:12
  390.7 9.0 %fusion.120 = (bf16[2048,768]{1,0:T(8,128)(2,1)S(1)}, f32[2048,768]{1,0:T(8,128)}) fusion(f32[2048,768]{1,0:T(8,128)} %param.14, f32[2048]{0:T(1024)S(1)} %convert_add_fusion, bf16[2048,768]{1,0:T(8,128)(2,1)} %reduce_sum.208, f32[2048]{0:T(1024)S(1)} %copy-done.7), kind=kLoop, calls=%fused_computation.222 | loop fusion | flops 7864320 | bytes 18890752 | tf_op jit(solution)/shard_map/convert_element_type | solution.py:81
  399.6 0.7 multiply_reduce_fusion.2
  400.3 4.0 select_reduce_fusion
  404.4 21.4 %all-reduce.4 = f32[1024]{0:T(1024)S(1)} all-reduce(f32[1024]{0:T(1024)S(1)} %add_select_fusion), channel_id=4, replica_groups=mesh['grp'=4,'tm'=8] {'tm'}, use_global_device_ids=true, to_apply=%region_22.23.clone | all-reduce | flops 1024 | bytes 8192
  425.7 0.6 fusion.118
  (48 shorter events, 0.5 us)
Async XLA Ops:
  7.2 240.0 %copy-start = (bf16[512,768]{1,0:T(8,128)(2,1)S(1)}, bf16[512,768]{1,0:T(8,128)(2,1)}, u32[]{:S(2)}) copy-start(bf16[512,768]{1,0:T(8,128)(2,1)} %param.13) | copy-start | bytes 2359300
  7.2 17.6 %copy-start.9 = (bf16[10,512]{1,0:T(8,128)(2,1)S(1)}, bf16[10,512]{1,0:T(8,128)(2,1)}, u32[]{:S(2)}) copy-start(bf16[10,512]{1,0:T(8,128)(2,1)} %param.10) | copy-start | bytes 30724
  7.2 287.0 %all-gather.5.cloned.1.call-start = ((), (), s32[]{:S(2)}) async-start(), calls=%async_computation | async-start | bytes 1769472 | tf_op jit(solution)/shard_map/all_gather | solution.py:85
  8.0 6.3 %collective-permute-start = (bf16[80]{0:T(256)(128)(2,1)S(1)}, bf16[80]{0:T(256)(128)(2,1)S(1)}, u32[]{:S(2)}, u32[]{:S(2)}) collective-permute-start(bf16[80]{0:T(256)(128)(2,1)S(1)} %slice_bitcast_fusion), channel_id=1, source_target_pairs={{1,0},{2,1},{3,2},{4,3},{5,4},{6,5},{7,6},{9,8},{10,9},{11,10},{12... | collective-permute-start | bytes 488 | tf_op jit(solution)/shard_map/ppermute | solution.py:18
  24.8 8.0 %copy-start.5 = (bf16[8207,5]{1,0:T(8,128)(2,1)S(1)}, bf16[8207,5]{1,0:T(8,128)(2,1)}, u32[]{:S(2)}) copy-start(bf16[8207,5]{1,0:T(8,128)(2,1)} %slice.149) | copy-start | bytes 246214
  43.7 10.7 %copy-start.1 = (f32[8207,512]{1,0:T(8,128)S(1)}, f32[8207,512]{1,0:T(8,128)}, u32[]{:S(2)}) copy-start(f32[8207,512]{1,0:T(8,128)} %get-tuple-element.10) | copy-start | bytes 50423812
  134.1 7.4 %copy-start.3 = (bf16[4104,1024]{1,0:T(8,128)(2,1)S(1)}, bf16[4104,1024]{1,0:T(8,128)(2,1)}, u32[]{:S(2)}) copy-start(bf16[4104,1024]{1,0:T(8,128)(2,1)} %reshape.165) | copy-start | bytes 25214980
  169.3 1.9 copy-start.2
  215.2 4.6 %copy-start.4 = (bf16[2052,512]{1,0:T(8,128)(2,1)S(1)}, bf16[2052,512]{1,0:T(8,128)(2,1)}, u32[]{:S(2)}) copy-start(bf16[2052,512]{1,0:T(8,128)(2,1)} %concatenate.18) | copy-start | bytes 6303748
  241.0 7.3 %copy-start.10 = (s32[1,128]{1,0:T(1,128)S(1)}, s32[1,128]{1,0:T(1,128)}, u32[]{:S(2)}) copy-start(s32[1,128]{1,0:T(1,128)} %param.9) | copy-start | bytes 1540
  248.2 133.4 %all-gather.7.cloned.1.call-start = ((), (), s32[]{:S(2)}) async-start(), calls=%async_computation.1 | async-start | bytes 15728640 | tf_op jit(solution)/shard_map/all_gather | solution.py:11
  294.2 6.4 %copy-start.11 = (u32[32]{0:T(128)S(1)}, u32[32]{0:T(128)}, u32[]{:S(2)}) copy-start(u32[32]{0:T(128)} %constant.31) | copy-start | bytes 388
  294.2 14.7 %copy-start.7 = (f32[2048]{0:T(1024)S(1)}, f32[2048]{0:T(1024)}, u32[]{:S(2)}) copy-start(f32[2048]{0:T(1024)} %param.15) | copy-start | bytes 24580
  300.6 8.4 %copy-start.6 = (bf16[1024,768]{1,0:T(8,128)(2,1)S(1)}, bf16[1024,768]{1,0:T(8,128)(2,1)}, u32[]{:S(2)}) copy-start(bf16[1024,768]{1,0:T(8,128)(2,1)} %all-gather.5.cloned.1.call-done) | copy-start | bytes 4718596
  309.0 81.7 %copy-start.8 = (f32[2048]{0:T(1024)}, f32[2048]{0:T(1024)S(1)}, u32[]{:S(2)}) copy-start(f32[2048]{0:T(1024)S(1)} %convert_add_fusion) | copy-start | bytes 24580
Sparse Core Ops, SparseCore 0:
  248.4 45.8 all-gather.4
  300.7 80.9 all-gather.6
